TPU v7x, 32 devices: a whole 2x2x4 slice. The times are simulated.
32 devices in a mesh: grp: 4 (over y, x), tp: 8 (over z, core).
Axes of the slice: x: 2, y: 2, z: 4, core: 2. Of those that a mesh axis runs over, the one named last changes fastest.
Arguments:
- batch_sizes: int32 [4], P('grp'), may hold values from 1 to 16
- seq_lens: int32 [4, 16], P('grp'), may hold values from 1 to 2048
- page_table: int32 [4, 16, 128], P('grp', None, 'tp'), may hold values from 0 to 255, as said below
- queries: bfloat16 [4, 16, 4096], P('grp', None, 'tp'), may hold values from -4 to 14
- kv_pool: bfloat16 [4, 2048, 16, 1024], P('grp', 'tp'), may hold values from -7 to 7
- new_kv: bfloat16 [4, 16, 1024], P('grp'), may hold values from -6 to 6
- out_weight: bfloat16 [4096, 2880], P('tp', 'grp'), may hold values from -0.375 to 0.375
Outputs:
- mixed: float32 [4, 16, 2880], P('grp')
Inputs may be any that keep to these rules, and one draw needn't show every extreme that they name: `batch_sizes`: slots below a group's batch size are live; the others are empty and their outputs are zero. `seq_lens`: entries of empty slots are drawn but unused. `page_table`: for every group g and every t, the entries [g, :, t * 16 to (t + 1) * 16 - 1] are a permutation of 0 to 255.
All inputs are finite; a program needn't handle non-finite values.
Results may differ from a plain program's by a relative error of at most 0.007.
Values may be sent and summed in bfloat16 or wider, within the bound.
A program may use at most 64 MiB of HBM per device.

v0:
```python
import jax
import jax.numpy as jnp
from jax import lax
from jax.sharding import PartitionSpec as P

HEADS = 64
KV_HEADS = 8
HD = 64
SLOT_BLOCK = 2
PRECISE = lax.Precision.HIGHEST
NEG_BIG = -1e30


def attend_slots(query_rows, page_blocks, lengths, tp_index, tp_count, kv_heads):
    slot_count, page_count, page_len, row_width = page_blocks.shape
    head_dim = row_width // (2 * kv_heads)
    head_count = query_rows.shape[1] // head_dim
    group_size = head_count // kv_heads
    token_count = page_count * page_len
    token_rows = page_blocks.reshape(slot_count, token_count, row_width)
    key_rows = token_rows[:, :, : row_width // 2].reshape(
        slot_count, token_count, kv_heads, head_dim
    )
    value_rows = token_rows[:, :, row_width // 2 :].reshape(
        slot_count, token_count, kv_heads, head_dim
    )
    grouped = query_rows.reshape(slot_count, kv_heads, group_size, head_dim)
    scores = jnp.einsum("skgd,stkd->skgt", grouped, key_rows, preferred_element_type=jnp.float32)
    scores = scores * head_dim ** (-0.5)
    page_index = lax.broadcasted_iota(jnp.int32, (page_count, page_len), 0)
    token_index = lax.broadcasted_iota(jnp.int32, (page_count, page_len), 1)
    position = ((page_index * tp_count + tp_index) * page_len + token_index).reshape(token_count)
    valid_mask = (position[None, :] < lengths[:, None])[:, None, None, :]
    scores = jnp.where(valid_mask, scores, NEG_BIG)
    top_score = jnp.max(scores, axis=3)
    weights = jnp.where(valid_mask, jnp.exp(scores - top_score[..., None]), 0.0)
    weight_sum = jnp.sum(weights, axis=3)
    weighted = jnp.einsum(
        "skgt,stkd->skgd",
        weights.astype(jnp.bfloat16),
        value_rows,
        preferred_element_type=jnp.float32,
    )
    return (
        weighted.reshape(slot_count, head_count * head_dim),
        top_score.reshape(slot_count, head_count),
        weight_sum.reshape(slot_count, head_count),
    )


def local(batch_sizes, seq_lens, page_table, queries, kv_pool, new_kv, out_weight):
    tp_count = lax.axis_size("tp")
    tp_index = lax.axis_index("tp")
    gathered = lax.all_gather(queries, "tp", axis=2, tiled=True)[0]
    kv_pages = kv_pool[0]
    page_ids = page_table[0]
    lengths = seq_lens[0]
    live_count = batch_sizes[0]
    slot_count, full_width = gathered.shape
    head_dim = HD
    head_count = HEADS
    slot_order = jnp.arange(slot_count, dtype=jnp.int32)

    def local_block(block_index, state):
        first_slot = block_index * SLOT_BLOCK
        query_rows = lax.dynamic_slice_in_dim(gathered, first_slot, SLOT_BLOCK, 0)
        block_ids = lax.dynamic_slice_in_dim(page_ids, first_slot, SLOT_BLOCK, 0)
        block_lengths = lax.dynamic_slice_in_dim(lengths, first_slot, SLOT_BLOCK, 0)
        block_slots = first_slot + jnp.arange(SLOT_BLOCK, dtype=jnp.int32)
        block_lengths = jnp.where(block_slots < live_count, block_lengths, 0)
        pieces = attend_slots(
            query_rows, kv_pages[block_ids], block_lengths, tp_index, tp_count, KV_HEADS
        )
        return tuple(
            (
                lax.dynamic_update_slice_in_dim(whole, piece, first_slot, 0)
                for whole, piece in zip(state, pieces)
            )
        )

    start_state = (
        jnp.zeros((slot_count, full_width), jnp.float32),
        jnp.full((slot_count, head_count), NEG_BIG, jnp.float32),
        jnp.zeros((slot_count, head_count), jnp.float32),
    )
    block_total = (live_count + SLOT_BLOCK - 1) // SLOT_BLOCK
    weighted, top_score, weight_sum = lax.fori_loop(0, block_total, local_block, start_state)
    own_heads = head_count // tp_count
    own_width = own_heads * head_dim
    shard_weighted, shard_top, shard_sum = (
        lax.all_to_all(weighted[None], "tp", split_axis=2, concat_axis=0, tiled=True),
        lax.all_to_all(top_score[None], "tp", split_axis=2, concat_axis=0, tiled=True),
        lax.all_to_all(weight_sum[None], "tp", split_axis=2, concat_axis=0, tiled=True),
    )
    part_top = jnp.max(shard_top, axis=0)
    shard_rescale = jnp.exp(shard_top - part_top[None])
    part_weighted = jnp.sum(shard_weighted * jnp.repeat(shard_rescale, head_dim, axis=-1), axis=0)
    part_sum = jnp.sum(shard_sum * shard_rescale, axis=0)
    fresh_rows = new_kv[0].astype(jnp.float32)
    kv_width = KV_HEADS * head_dim
    new_keys = fresh_rows[:, :kv_width].reshape(slot_count, KV_HEADS, head_dim)
    new_values = fresh_rows[:, kv_width:].reshape(slot_count, KV_HEADS, head_dim)
    head_ids = tp_index * own_heads + jnp.arange(own_heads, dtype=jnp.int32)
    head_map = (
        head_ids[:, None] // (head_count // KV_HEADS)
        == jnp.arange(KV_HEADS, dtype=jnp.int32)[None, :]
    ).astype(jnp.float32)
    own_keys = jnp.einsum("jk,skd->sjd", head_map, new_keys, precision=PRECISE)
    own_values = jnp.einsum("jk,skd->sjd", head_map, new_values, precision=PRECISE)
    own_queries = queries[0].astype(jnp.float32).reshape(slot_count, own_heads, head_dim)
    self_score = jnp.sum(own_queries * own_keys, axis=-1) * head_dim ** (-0.5)
    final_top = jnp.maximum(part_top, self_score)
    cache_rescale = jnp.exp(part_top - final_top)
    self_rescale = jnp.exp(self_score - final_top)
    numerator = part_weighted.reshape(slot_count, own_heads, head_dim) * cache_rescale[..., None]
    numerator = numerator + own_values * self_rescale[..., None]
    denominator = part_sum * cache_rescale + self_rescale
    attended = (numerator / denominator[..., None]).reshape(slot_count, own_width)
    attended = jnp.where((slot_order < live_count)[:, None], attended, 0.0).astype(jnp.bfloat16)
    projected = jnp.dot(
        attended,
        lax.all_gather(out_weight, "grp", axis=1, tiled=True),
        preferred_element_type=jnp.float32,
    )
    mixed = lax.psum(projected, "tp")
    return mixed[None]


def solution(mesh):
    return jax.shard_map(
        local,
        mesh=mesh,
        in_specs=(
            P("grp"),
            P("grp", None),
            P("grp", None, "tp"),
            P("grp", None, "tp"),
            P("grp", "tp", None, None),
            P("grp", None, None),
            P("tp", "grp"),
        ),
        out_specs=P("grp", None, None),
        check_vma=False,
    )
```

profile of v0, /device:TPU:0, one launch (start us, length us, event | category | flops | bytes accessed | tf_op | source)
XLA Modules:
  0.0 214.4 jit_solution(14500293375372935720)
XLA Ops:
  6.5 0.7 all-gather.2.cloned.1.call-update
  7.9 15.9 %all_gather.6 = bf16[1,16,4096]{2,1,0:T(8,128)(2,1)S(1)} all-gather(bf16[1,16,512]{2,1,0:T(8,128)(2,1)} %param.12), channel_id=1, replica_groups=mesh['grp'=4,'tp'=8] {'tp'}, dimensions={2}, use_global_device_ids=true | all-gather | bytes 147456 | tf_op jit(solution)/shard_map/all_gather | solution.py:54
  23.9 65.7 %while.14 = (s32[]{:T(128)}, f32[16,4096]{1,0:T(8,128)S(1)}, f32[16,64]{1,0:T(8,128)S(1)}, f32[16,64]{1,0:T(8,128)S(1)}, s32[]{:T(128)}, /*index=5*/s32[]{:T(128...) while((s32[]{:T(128)}, f32[16,4096]{1,0:T(8,128)S(1)}, ...), condition=%wide.region_3.4_spmd, body=%wide.region_0.3_spmd.sunk | while | flops 8685212 | bytes 7998579 | solution.py:87
  24.0 1.4 compare_select_fusion.8
  26.4 4.0 %gather_fusion = bf16[32,16,1024]{2,1,0:T(8,128)(2,1)S(1)} fusion(bf16[256,16,1024]{2,1,0:T(8,128)(2,1)} %get-tuple-element.223, s32[1024]{0:T(1024)S(1)} %pad_clamp_fusion.2), kind=kCustom, calls=%fused_computation.clone.1 | custom fusion | bytes 2097280 | tf_op jit(solution)/shard_map/while/body/gather | solution.py:72
  32.1 1.4 compare_select_fusion.8
  34.5 4.5 %gather_fusion = bf16[32,16,1024]{2,1,0:T(8,128)(2,1)S(1)} fusion(bf16[256,16,1024]{2,1,0:T(8,128)(2,1)} %get-tuple-element.223, s32[1024]{0:T(1024)S(1)} %pad_clamp_fusion.2), kind=kCustom, calls=%fused_computation.clone.1 | custom fusion | bytes 2097280 | tf_op jit(solution)/shard_map/while/body/gather | solution.py:72
  40.8 1.4 compare_select_fusion.8
  43.2 4.0 %gather_fusion = bf16[32,16,1024]{2,1,0:T(8,128)(2,1)S(1)} fusion(bf16[256,16,1024]{2,1,0:T(8,128)(2,1)} %get-tuple-element.223, s32[1024]{0:T(1024)S(1)} %pad_clamp_fusion.2), kind=kCustom, calls=%fused_computation.clone.1 | custom fusion | bytes 2097280 | tf_op jit(solution)/shard_map/while/body/gather | solution.py:72
  48.9 1.4 compare_select_fusion.8
  51.3 4.0 %gather_fusion = bf16[32,16,1024]{2,1,0:T(8,128)(2,1)S(1)} fusion(bf16[256,16,1024]{2,1,0:T(8,128)(2,1)} %get-tuple-element.223, s32[1024]{0:T(1024)S(1)} %pad_clamp_fusion.2), kind=kCustom, calls=%fused_computation.clone.1 | custom fusion | bytes 2097280 | tf_op jit(solution)/shard_map/while/body/gather | solution.py:72
  57.0 1.4 compare_select_fusion.8
  59.5 4.0 %gather_fusion = bf16[32,16,1024]{2,1,0:T(8,128)(2,1)S(1)} fusion(bf16[256,16,1024]{2,1,0:T(8,128)(2,1)} %get-tuple-element.223, s32[1024]{0:T(1024)S(1)} %pad_clamp_fusion.2), kind=kCustom, calls=%fused_computation.clone.1 | custom fusion | bytes 2097280 | tf_op jit(solution)/shard_map/while/body/gather | solution.py:72
  65.2 1.4 compare_select_fusion.8
  67.6 4.0 %gather_fusion = bf16[32,16,1024]{2,1,0:T(8,128)(2,1)S(1)} fusion(bf16[256,16,1024]{2,1,0:T(8,128)(2,1)} %get-tuple-element.223, s32[1024]{0:T(1024)S(1)} %pad_clamp_fusion.2), kind=kCustom, calls=%fused_computation.clone.1 | custom fusion | bytes 2097280 | tf_op jit(solution)/shard_map/while/body/gather | solution.py:72
  73.3 1.4 compare_select_fusion.8
  75.7 4.0 %gather_fusion = bf16[32,16,1024]{2,1,0:T(8,128)(2,1)S(1)} fusion(bf16[256,16,1024]{2,1,0:T(8,128)(2,1)} %get-tuple-element.223, s32[1024]{0:T(1024)S(1)} %pad_clamp_fusion.2), kind=kCustom, calls=%fused_computation.clone.1 | custom fusion | bytes 2097280 | tf_op jit(solution)/shard_map/while/body/gather | solution.py:72
  81.5 1.4 compare_select_fusion.8
  83.9 4.0 %gather_fusion = bf16[32,16,1024]{2,1,0:T(8,128)(2,1)S(1)} fusion(bf16[256,16,1024]{2,1,0:T(8,128)(2,1)} %get-tuple-element.223, s32[1024]{0:T(1024)S(1)} %pad_clamp_fusion.2), kind=kCustom, calls=%fused_computation.clone.1 | custom fusion | bytes 2097280 | tf_op jit(solution)/shard_map/while/body/gather | solution.py:72
  91.6 4.6 %all-to-all-start.1 = ((f32[8,1,128]{2,1,0:T(1,128)}), f32[8,1,128]{2,1,0:T(1,128)S(1)}, u32[]{:S(2)}, u32[]{:S(2)}) async-start(f32[8,1,128]{2,1,0:T(1,128)} %reshape.169), calls=%async_computation.1 | async-start | bytes 8192 | tf_op jit(solution)/shard_map/all_to_all | solution.py:92
  96.4 0.7 reduce.3
  97.9 3.9 %all-to-all-done.1 = f32[8,1,128]{2,1,0:T(1,128)S(1)} async-done(((f32[8,1,128]{2,1,0:T(1,128)}), f32[8,1,128]{2,1,0:T(1,128)S(1)}, u32[]{:S(2)}, u32[]{:S(2)}) %all-to-all-start.1) | async-done | bytes 4128 | tf_op jit(solution)/shard_map/all_to_all | solution.py:92
  101.8 3.3 %all-to-all-start.2 = ((f32[8,1,128]{2,1,0:T(1,128)}), f32[8,1,128]{2,1,0:T(1,128)S(1)}, u32[]{:S(2)}, u32[]{:S(2)}) async-start(f32[8,1,128]{2,1,0:T(1,128)} %reshape.171), calls=%async_computation.2 | async-start | bytes 8192 | tf_op jit(solution)/shard_map/all_to_all | solution.py:93
  106.0 19.3 %reduce.1 = f32[4096,16]{1,0:T(8,128)} reduce(f32[4096,1,16]{2,1,0:T(1,128)S(1)} %bitcast.84, f32[]{:T(128)} %broadcast.132), dimensions={1}, to_apply=%bitcast.54.reduce_sub_computation | reduce | bytes 524292
  125.3 3.0 %reshape.167 = f32[8,1,8192]{2,1,0:T(1,128)} reshape(f32[4096,16]{1,0:T(8,128)} %reduce.1) | data formatting | bytes 524288
  128.3 5.0 %all-to-all-start = ((f32[8,1,8192]{2,1,0:T(1,128)}), f32[8,1,8192]{2,1,0:T(1,128)S(1)}, u32[]{:S(2)}, u32[]{:S(2)}) async-start(f32[8,1,8192]{2,1,0:T(1,128)} %reshape.167), calls=%async_computation | async-start | bytes 524288 | tf_op jit(solution)/shard_map/all_to_all | solution.py:91
  135.5 7.5 %all-to-all-done = f32[8,1,8192]{2,1,0:T(1,128)S(1)} async-done(((f32[8,1,8192]{2,1,0:T(1,128)}), f32[8,1,8192]{2,1,0:T(1,128)S(1)}, u32[]{:S(2)}, u32[]{:S(2)}) %all-to-all-start) | async-done | bytes 262176 | tf_op jit(solution)/shard_map/all_to_all | solution.py:91
  143.1 1.2 reduce.2
  144.3 3.9 %reshape.168 = f32[4096,1,16]{2,1,0:T(1,128)S(1)} reshape(f32[8,8192]{1,0:T(8,128)S(1)} %reduce.2) | data formatting | bytes 524288
  149.0 3.4 %convolution_bitcast_fusion = f32[1,16,2880]{2,1,0:T(8,128)} fusion(bf16[512,2880]{0,1:T(8,128)(2,1)} %all-gather.2.cloned.1.call-done, bf16[16,512]{1,0:T(8,128)(2,1)S(1)} %reshape.153, pred[16]{0:T(512)(128)(4,1)S(1)} %iota_compare_fusion.1), kind=kOutput, calls=%fused_computation.22 | convolution fusion | flops 47194112 | bytes 3149840 | tf_op jit(solution)/shard_map/dot_general | solution.py:120
  152.4 53.6 %all-reduce.2.cloned.1.call-done = f32[1,16,2880]{2,1,0:T(8,128)} async-done(((f32[1,16,2880]{2,1,0:T(8,128)}), f32[1,16,2880]{2,1,0:T(8,128)}) %all-reduce.2.cloned.1.call-update) | async-done | bytes 184336 | tf_op jit(solution)/shard_map/psum | solution.py:125
  206.0 1.6 copy.58
  (201 shorter events, 28.2 us)
Async XLA Ops:
  6.5 142.4 %all-gather.2.cloned.1.call-start = ((), (), s32[]{:S(2)}) async-start(), calls=%async_computation.3 | async-start | bytes 3686400 | tf_op jit(solution)/shard_map/all_gather | solution.py:122
  23.9 72.3 %copy-start.1 = (bf16[1,16,1024]{2,1,0:T(8,128)(2,1)S(1)}, bf16[1,16,1024]{2,1,0:T(8,128)(2,1)}, u32[]{:S(2)}) copy-start(bf16[1,16,1024]{2,1,0:T(8,128)(2,1)} %param.14) | copy-start | bytes 98308
  23.9 72.3 %copy-start = (bf16[1,16,512]{2,1,0:T(8,128)(2,1)S(1)}, bf16[1,16,512]{2,1,0:T(8,128)(2,1)}, u32[]{:S(2)}) copy-start(bf16[1,16,512]{2,1,0:T(8,128)(2,1)} %param.12) | copy-start | bytes 49156
  91.6 10.2 %all-to-all-start.1 = ((f32[8,1,128]{2,1,0:T(1,128)}), f32[8,1,128]{2,1,0:T(1,128)S(1)}, u32[]{:S(2)}, u32[]{:S(2)}) async-start(f32[8,1,128]{2,1,0:T(1,128)} %reshape.169), calls=%async_computation.1 | async-start | bytes 8192 | tf_op jit(solution)/shard_map/all_to_all | solution.py:92
  101.8 26.5 %all-to-all-start.2 = ((f32[8,1,128]{2,1,0:T(1,128)}), f32[8,1,128]{2,1,0:T(1,128)S(1)}, u32[]{:S(2)}, u32[]{:S(2)}) async-start(f32[8,1,128]{2,1,0:T(1,128)} %reshape.171), calls=%async_computation.2 | async-start | bytes 8192 | tf_op jit(solution)/shard_map/all_to_all | solution.py:93
  128.3 14.7 %all-to-all-start = ((f32[8,1,8192]{2,1,0:T(1,128)}), f32[8,1,8192]{2,1,0:T(1,128)S(1)}, u32[]{:S(2)}, u32[]{:S(2)}) async-start(f32[8,1,8192]{2,1,0:T(1,128)} %reshape.167), calls=%async_computation | async-start | bytes 524288 | tf_op jit(solution)/shard_map/all_to_all | solution.py:91
  133.4 72.6 %all-reduce.2.cloned.1.call-start = ((), (), s32[]{:S(2)}) async-start(), calls=%async_computation.4 | async-start | bytes 376832 | tf_op jit(solution)/shard_map/psum | solution.py:125
Sparse Core Ops, SparseCore 0:
  9.2 44.9 all-gather.1
  152.5 53.4 all-reduce.1
where the time goes:
time: 216 us; the launch traced here: 214 us
  waiting for transfers between devices  65.8 us (30%)
  local copies, waits for them, and re-layouts  53.4 us (25%)
  other arithmetic  42.9 us (20%)
  blocking collectives  15.9 us (7%)
  between operations  14.3 us (7%)
  starting transfers between devices  13.2 us (6%)
  matrix products  8.29 us (4%)
    psum x1, waiting for transfers between devices, local(): mixed = lax.psum(projected, 'tp')  53.6 us
    gather x8, local copies, waits for them, and re-layouts, local_block(): kv_pages[block_ids]  32.4 us
    unnamed x3, other arithmetic  20.7 us
    all_gather x1, blocking collectives, local(): gathered = lax.all_gather(queries, 'tp', axis=2, tiled=True)[0]  15.9 us
    select_n x8, other arithmetic, local_block(): block_lengths = jnp.where(block_slots < live_count, block_lengths, 0)  11 us
    unnamed x12, local copies, waits for them, and re-layouts  10.6 us
    all_to_all x1, waiting for transfers between devices, local(): lax.all_to_all(weighted[None], 'tp', split_axis=2, concat_axis=0, tiled=T...  7.53 us
    select_n x8, other arithmetic, local_block(): kv_pages[block_ids]  5.57 us
  transfers between devices with their start and end apart: 5, of which 3 were waited for; matrix products, arithmetic and copies ran while one was open for 46% of the time, Pallas kernels for 0%

commit v1 on v0

--- a/solution.py
+++ b/solution.py
@@ -88,7 +88,12 @@
     own_heads = head_count // tp_count
     own_width = own_heads * head_dim
     shard_weighted, shard_top, shard_sum = (
-        lax.all_to_all(weighted[None], "tp", split_axis=2, concat_axis=0, tiled=True),
+        jnp.concatenate(
+            lax.all_to_all(
+                jnp.stack(jnp.split(weighted[None], lax.axis_size("tp"), axis=2)), "tp", 0, 0
+            ),
+            axis=0,
+        ),
         lax.all_to_all(top_score[None], "tp", split_axis=2, concat_axis=0, tiled=True),
         lax.all_to_all(weight_sum[None], "tp", split_axis=2, concat_axis=0, tiled=True),
     )

time: 216 us -> 194 us (0.90)
  other arithmetic: 42.9 us -> 22.3 us
  local copies, waits for them, and re-layouts: 53.4 us -> 51.2 us
    unnamed x3 -> x2, other arithmetic: 20.7 us -> 1.51 us
    all_to_all x1, waiting for transfers between devices: 0.01 us -> 5.23 us  [local(): lax.all_to_all(weight_sum[None], 'tp', split_axis=2, concat_axis=0, tiled...]
    all_to_all x1, waiting for transfers between devices: 3.89 us -> 0.01 us  [local(): lax.all_to_all(top_score[None], 'tp', split_axis=2, concat_axis=0, tiled=...]
    unnamed x12 -> x17, local copies, waits for them, and re-layouts: 10.6 us -> 8 us
  transfers between devices with their start and end apart: 5 -> 5, of which waited for: 3 -> 3; matrix products, arithmetic and copies ran while one was open for 46% -> 40% of each run, Pallas kernels for 0% -> 0%
where the time goes in v1:
time: 194 us; the launch traced here: 192 us
  waiting for transfers between devices  66.6 us (34%)
  local copies, waits for them, and re-layouts  51.2 us (26%)
  other arithmetic  22.3 us (11%)
  blocking collectives  15.9 us (8%)
  between operations  14.3 us (7%)
  starting transfers between devices  13.2 us (7%)
  matrix products  8.29 us (4%)
    psum x1, waiting for transfers between devices, local(): mixed = lax.psum(projected, 'tp')  53.6 us
    gather x8, local copies, waits for them, and re-layouts, local_block(): kv_pages[block_ids]  32.4 us
    all_gather x1, blocking collectives, local(): gathered = lax.all_gather(queries, 'tp', axis=2, tiled=True)[0]  15.9 us
    select_n x8, other arithmetic, local_block(): block_lengths = jnp.where(block_slots < live_count, block_lengths, 0)  11 us
    unnamed x17, local copies, waits for them, and re-layouts  8 us
    all_to_all x1, waiting for transfers between devices, local(): lax.all_to_all(jnp.stack(jnp.split(weighted[None], lax.axis_size('tp'), a...  7.09 us
    select_n x8, other arithmetic, local_block(): kv_pages[block_ids]  5.57 us
    all_to_all x1, waiting for transfers between devices, local(): lax.all_to_all(weight_sum[None], 'tp', split_axis=2, concat_axis=0, tiled...  5.23 us
  transfers between devices with their start and end apart: 5, of which 3 were waited for; matrix products, arithmetic and copies ran while one was open for 40% of the time, Pallas kernels for 0%

profile of v1, /device:TPU:0, one launch (start us, length us, event | category | flops | bytes accessed | tf_op | source)
XLA Modules:
  0.0 192.4 jit_solution(4684572021217526752)
XLA Ops:
  6.5 0.7 all-gather.2.cloned.1.call-update
  7.9 15.9 %all_gather.6 = bf16[1,16,4096]{2,1,0:T(8,128)(2,1)S(1)} all-gather(bf16[1,16,512]{2,1,0:T(8,128)(2,1)} %param.12), channel_id=1, replica_groups=mesh['grp'=4,'tp'=8] {'tp'}, dimensions={2}, use_global_device_ids=true | all-gather | bytes 147456 | tf_op jit(solution)/shard_map/all_gather | solution.py:54
  23.9 65.7 %while.14 = (s32[]{:T(128)}, f32[16,4096]{1,0:T(8,128)S(1)}, f32[16,64]{1,0:T(8,128)S(1)}, f32[16,64]{1,0:T(8,128)S(1)}, s32[]{:T(128)}, /*index=5*/s32[]{:T(128...) while((s32[]{:T(128)}, f32[16,4096]{1,0:T(8,128)S(1)}, ...), condition=%wide.region_3.4_spmd, body=%wide.region_0.3_spmd.sunk | while | flops 8685212 | bytes 7998579 | solution.py:87
  24.0 1.4 compare_select_fusion.8
  25.6 0.7 compare_select_fusion.7
  26.4 4.0 %gather_fusion = bf16[32,16,1024]{2,1,0:T(8,128)(2,1)S(1)} fusion(bf16[256,16,1024]{2,1,0:T(8,128)(2,1)} %get-tuple-element.223, s32[1024]{0:T(1024)S(1)} %pad_clamp_fusion.2), kind=kCustom, calls=%fused_computation.clone.1 | custom fusion | bytes 2097280 | tf_op jit(solution)/shard_map/while/body/gather | solution.py:72
  32.1 1.4 compare_select_fusion.8
  33.7 0.7 compare_select_fusion.7
  34.5 4.5 %gather_fusion = bf16[32,16,1024]{2,1,0:T(8,128)(2,1)S(1)} fusion(bf16[256,16,1024]{2,1,0:T(8,128)(2,1)} %get-tuple-element.223, s32[1024]{0:T(1024)S(1)} %pad_clamp_fusion.2), kind=kCustom, calls=%fused_computation.clone.1 | custom fusion | bytes 2097280 | tf_op jit(solution)/shard_map/while/body/gather | solution.py:72
  40.8 1.4 compare_select_fusion.8
  43.2 4.0 %gather_fusion = bf16[32,16,1024]{2,1,0:T(8,128)(2,1)S(1)} fusion(bf16[256,16,1024]{2,1,0:T(8,128)(2,1)} %get-tuple-element.223, s32[1024]{0:T(1024)S(1)} %pad_clamp_fusion.2), kind=kCustom, calls=%fused_computation.clone.1 | custom fusion | bytes 2097280 | tf_op jit(solution)/shard_map/while/body/gather | solution.py:72
  48.9 1.4 compare_select_fusion.8
  51.3 4.0 %gather_fusion = bf16[32,16,1024]{2,1,0:T(8,128)(2,1)S(1)} fusion(bf16[256,16,1024]{2,1,0:T(8,128)(2,1)} %get-tuple-element.223, s32[1024]{0:T(1024)S(1)} %pad_clamp_fusion.2), kind=kCustom, calls=%fused_computation.clone.1 | custom fusion | bytes 2097280 | tf_op jit(solution)/shard_map/while/body/gather | solution.py:72
  57.0 1.4 compare_select_fusion.8
  58.7 0.7 compare_select_fusion.7
  59.5 4.0 %gather_fusion = bf16[32,16,1024]{2,1,0:T(8,128)(2,1)S(1)} fusion(bf16[256,16,1024]{2,1,0:T(8,128)(2,1)} %get-tuple-element.223, s32[1024]{0:T(1024)S(1)} %pad_clamp_fusion.2), kind=kCustom, calls=%fused_computation.clone.1 | custom fusion | bytes 2097280 | tf_op jit(solution)/shard_map/while/body/gather | solution.py:72
  65.2 1.4 compare_select_fusion.8
  67.6 4.0 %gather_fusion = bf16[32,16,1024]{2,1,0:T(8,128)(2,1)S(1)} fusion(bf16[256,16,1024]{2,1,0:T(8,128)(2,1)} %get-tuple-element.223, s32[1024]{0:T(1024)S(1)} %pad_clamp_fusion.2), kind=kCustom, calls=%fused_computation.clone.1 | custom fusion | bytes 2097280 | tf_op jit(solution)/shard_map/while/body/gather | solution.py:72
  73.3 1.4 compare_select_fusion.8
  75.7 4.0 %gather_fusion = bf16[32,16,1024]{2,1,0:T(8,128)(2,1)S(1)} fusion(bf16[256,16,1024]{2,1,0:T(8,128)(2,1)} %get-tuple-element.223, s32[1024]{0:T(1024)S(1)} %pad_clamp_fusion.2), kind=kCustom, calls=%fused_computation.clone.1 | custom fusion | bytes 2097280 | tf_op jit(solution)/shard_map/while/body/gather | solution.py:72
  81.5 1.4 compare_select_fusion.8
  83.9 4.0 %gather_fusion = bf16[32,16,1024]{2,1,0:T(8,128)(2,1)S(1)} fusion(bf16[256,16,1024]{2,1,0:T(8,128)(2,1)} %get-tuple-element.223, s32[1024]{0:T(1024)S(1)} %pad_clamp_fusion.2), kind=kCustom, calls=%fused_computation.clone.1 | custom fusion | bytes 2097280 | tf_op jit(solution)/shard_map/while/body/gather | solution.py:72
  90.3 0.8 reduce.3
  91.7 4.6 %all-to-all-start.1 = ((f32[8,1,128]{2,1,0:T(1,128)}), f32[8,1,128]{2,1,0:T(1,128)S(1)}, u32[]{:S(2)}, u32[]{:S(2)}) async-start(f32[8,1,128]{2,1,0:T(1,128)} %reshape.171), calls=%async_computation.1 | async-start | bytes 8192 | tf_op jit(solution)/shard_map/all_to_all | solution.py:97
  101.4 0.8 reduce.1
  102.9 5.1 %all-to-all-start.2 = ((f32[8,1,128]{2,1,0:T(1,128)}), f32[8,1,128]{2,1,0:T(1,128)S(1)}, u32[]{:S(2)}, u32[]{:S(2)}) async-start(f32[8,1,128]{2,1,0:T(1,128)} %reshape.173), calls=%async_computation.2 | async-start | bytes 8192 | tf_op jit(solution)/shard_map/all_to_all | solution.py:98
  108.3 5.2 %all-to-all-done.2 = f32[8,1,128]{2,1,0:T(1,128)S(1)} async-done(((f32[8,1,128]{2,1,0:T(1,128)}), f32[8,1,128]{2,1,0:T(1,128)S(1)}, u32[]{:S(2)}, u32[]{:S(2)}) %all-to-all-start.2) | async-done | bytes 4128 | tf_op jit(solution)/shard_map/all_to_all | solution.py:98
  113.5 3.4 %all-to-all-start = ((f32[8,1,16,512]{3,2,1,0:T(8,128)}), f32[8,1,16,512]{3,2,1,0:T(8,128)S(1)}, u32[]{:S(2)}, u32[]{:S(2)}) async-start(f32[8,1,16,512]{3,2,1,0:T(8,128)} %fusion.15), calls=%async_computation | async-start | bytes 524288 | tf_op jit(solution)/shard_map/all_to_all | solution.py:92
  119.5 7.1 %all-to-all-done = f32[8,1,16,512]{3,2,1,0:T(8,128)S(1)} async-done(((f32[8,1,16,512]{3,2,1,0:T(8,128)}), f32[8,1,16,512]{3,2,1,0:T(8,128)S(1)}, u32[]{:S(2)}, u32[]{:S(2)}) %all-to-all-start) | async-done | bytes 262176 | tf_op jit(solution)/shard_map/all_to_all | solution.py:92
  127.0 3.4 %convolution_bitcast_fusion = f32[1,16,2880]{2,1,0:T(8,128)} fusion(bf16[512,2880]{0,1:T(8,128)(2,1)} %all-gather.2.cloned.1.call-done, bf16[16,512]{1,0:T(8,128)(2,1)S(1)} %reshape.157, pred[16]{0:T(512)(128)(4,1)S(1)} %iota_compare_fusion.1), kind=kOutput, calls=%fused_computation.22 | convolution fusion | flops 47194112 | bytes 3149840 | tf_op jit(solution)/shard_map/dot_general | solution.py:125
  130.4 53.6 %all-reduce.2.cloned.1.call-done = f32[1,16,2880]{2,1,0:T(8,128)} async-done(((f32[1,16,2880]{2,1,0:T(8,128)}), f32[1,16,2880]{2,1,0:T(8,128)}) %all-reduce.2.cloned.1.call-update) | async-done | bytes 184336 | tf_op jit(solution)/shard_map/psum | solution.py:130
  184.0 1.6 copy.64
  (207 shorter events, 29.8 us)
Async XLA Ops:
  6.5 120.5 %all-gather.2.cloned.1.call-start = ((), (), s32[]{:S(2)}) async-start(), calls=%async_computation.3 | async-start | bytes 3686400 | tf_op jit(solution)/shard_map/all_gather | solution.py:127
  23.9 72.4 %copy-start.1 = (bf16[1,16,1024]{2,1,0:T(8,128)(2,1)S(1)}, bf16[1,16,1024]{2,1,0:T(8,128)(2,1)}, u32[]{:S(2)}) copy-start(bf16[1,16,1024]{2,1,0:T(8,128)(2,1)} %param.14) | copy-start | bytes 98308
  23.9 77.3 %copy-start = (bf16[1,16,512]{2,1,0:T(8,128)(2,1)S(1)}, bf16[1,16,512]{2,1,0:T(8,128)(2,1)}, u32[]{:S(2)}) copy-start(bf16[1,16,512]{2,1,0:T(8,128)(2,1)} %param.12) | copy-start | bytes 49156
  91.7 11.2 %all-to-all-start.1 = ((f32[8,1,128]{2,1,0:T(1,128)}), f32[8,1,128]{2,1,0:T(1,128)S(1)}, u32[]{:S(2)}, u32[]{:S(2)}) async-start(f32[8,1,128]{2,1,0:T(1,128)} %reshape.171), calls=%async_computation.1 | async-start | bytes 8192 | tf_op jit(solution)/shard_map/all_to_all | solution.py:97
  102.9 10.6 %all-to-all-start.2 = ((f32[8,1,128]{2,1,0:T(1,128)}), f32[8,1,128]{2,1,0:T(1,128)S(1)}, u32[]{:S(2)}, u32[]{:S(2)}) async-start(f32[8,1,128]{2,1,0:T(1,128)} %reshape.173), calls=%async_computation.2 | async-start | bytes 8192 | tf_op jit(solution)/shard_map/all_to_all | solution.py:98
  113.5 13.1 %all-to-all-start = ((f32[8,1,16,512]{3,2,1,0:T(8,128)}), f32[8,1,16,512]{3,2,1,0:T(8,128)S(1)}, u32[]{:S(2)}, u32[]{:S(2)}) async-start(f32[8,1,16,512]{3,2,1,0:T(8,128)} %fusion.15), calls=%async_computation | async-start | bytes 524288 | tf_op jit(solution)/shard_map/all_to_all | solution.py:92
  116.9 67.1 %all-reduce.2.cloned.1.call-start = ((), (), s32[]{:S(2)}) async-start(), calls=%async_computation.4 | async-start | bytes 376832 | tf_op jit(solution)/shard_map/psum | solution.py:130
Sparse Core Ops, SparseCore 0:
  9.2 44.9 all-gather.1
  130.6 53.3 all-reduce.1
